TPU v7x, 512 devices: a whole 4x4x16 slice. The times are simulated.
512 devices in a mesh: cell: 32 (over z, y_lo), gene: 16 (over x, y_hi, core).
Axes of the slice: x: 4, y: 4 (y_hi: 2, y_lo: 2; y = y_hi * 2 + y_lo), z: 16, core: 2. Of those that a mesh axis runs over, the one named last changes fastest.
Arguments:
- counts: int32 [32768, 16384], P('cell', 'gene'), may hold values from 0 to 4
- factors: float32 [32768, 64], P(('cell', 'gene')), may hold values from -1.5 to 1.5
- loadings: float32 [16384, 64], P(('gene', 'cell')), may hold values from -1.5 to 1.5
- cell_offset: float32 [32768], P('cell'), may hold values from -1.2 to 1.2
- gene_offset: float32 [16384], P('gene'), may hold values from -1.2 to 1.2
Outputs:
- new_factors: float32 [32768, 64], P(('cell', 'gene'))
- new_loadings: float32 [16384, 64], P(('gene', 'cell'))
All inputs are finite; a program needn't handle non-finite values.
Results may differ from a plain program's by a relative error of at most 0.0003.
Values sent between devices are 32-bit elements; how exact they have to be, the bound alone decides.
A program may use at most 64 MiB of HBM per device.

v0:
```python
import jax
import jax.numpy as jnp
from jax import lax
from jax.sharding import PartitionSpec as P

ITERS = 2


epsilon = 1e-06
step_cap = 0.25


def bounded(ratio):
    return step_cap * jnp.tanh(ratio / step_cap)


def predict(factor_rows, loading_rows, cell_part, gene_part, count_part):
    linear = jnp.dot(
        factor_rows,
        loading_rows.T,
        preferred_element_type=jnp.float32,
        precision=lax.Precision.HIGHEST,
    )
    linear = linear + cell_part[:, None] + gene_part[None, :]
    means = jnp.exp(linear)
    excess = means - count_part.astype(jnp.float32)
    return (means, excess)


def per_device(counts, factors, loadings, cell_offset, gene_offset):
    rank = factors.shape[1]
    factor_block = lax.all_gather(factors, "gene", axis=0, tiled=True)
    loading_block = lax.all_gather(loadings, "cell", axis=0, tiled=True)
    own_u = factors
    own_v = loadings
    for iteration in range(ITERS):
        factor_rows = factor_block
        factor_means, factor_excess = predict(
            factor_rows, loading_block, cell_offset, gene_offset, counts
        )
        grad_u = jnp.dot(
            factor_excess,
            loading_block,
            preferred_element_type=jnp.float32,
            precision=lax.Precision.HIGHEST,
        )
        curv_u = jnp.dot(
            factor_means,
            loading_block * loading_block,
            preferred_element_type=jnp.float32,
            precision=lax.Precision.HIGHEST,
        )
        shares = lax.psum_scatter(
            jnp.concatenate([grad_u, curv_u], axis=1), "gene", scatter_dimension=0, tiled=True
        )
        own_u = own_u - bounded(shares[:, :rank] / (shares[:, rank:] + epsilon))
        factor_block = lax.all_gather(own_u, "gene", axis=0, tiled=True)
        loading_rows = loading_block
        means, excess = predict(factor_block, loading_rows, cell_offset, gene_offset, counts)
        contract = (((0,), (0,)), ((), ()))
        grad_v = lax.dot_general(
            excess,
            factor_block,
            contract,
            precision=lax.Precision.HIGHEST,
            preferred_element_type=jnp.float32,
        )
        curv_v = lax.dot_general(
            means,
            factor_block * factor_block,
            contract,
            precision=lax.Precision.HIGHEST,
            preferred_element_type=jnp.float32,
        )
        shares = lax.psum_scatter(
            jnp.concatenate([grad_v, curv_v], axis=1), "cell", scatter_dimension=0, tiled=True
        )
        own_v = own_v - bounded(shares[:, :rank] / (shares[:, rank:] + epsilon))
        if iteration + 1 < ITERS:
            loading_block = lax.all_gather(own_v, "cell", axis=0, tiled=True)
    return (own_u, own_v)


def solution(mesh):
    in_specs = (
        P("cell", "gene"),
        P(("cell", "gene"), None),
        P(("gene", "cell"), None),
        P("cell"),
        P("gene"),
    )
    out_specs = (P(("cell", "gene"), None), P(("gene", "cell"), None))
    return jax.shard_map(
        per_device, mesh=mesh, in_specs=in_specs, out_specs=out_specs, check_vma=False
    )
```

profile of v0, /device:TPU:2, one launch (start us, length us, event | category | flops | bytes accessed | tf_op | source)
XLA Modules:
  0.0 712.7 jit_solution(11519586317237446472)
XLA Ops:
  7.2 72.5 %all_gather.16 = f32[1024,64]{1,0:T(8,128)S(1)} all-gather(f32[32,64]{1,0:T(8,128)} %param.7), channel_id=1, replica_groups=mesh['cell'=32,'gene'=16] {'cell'}, dimensions={0}, use_global_device_ids=true | all-gather | bytes 270336 | tf_op jit(solution)/shard_map/all_gather | solution.py:33
  79.7 23.0 %all_gather.15 = f32[1024,64]{1,0:T(8,128)S(1)} all-gather(f32[64,64]{1,0:T(8,128)} %param.6), channel_id=1, replica_groups=mesh['cell'=32,'gene'=16] {'gene'}, dimensions={0}, use_global_device_ids=true | all-gather | bytes 278528 | tf_op jit(solution)/shard_map/all_gather | solution.py:32
  102.7 3.6 fusion.40
  106.3 4.9 fusion.12
  111.2 5.3 fusion.6
  116.5 1.0 copy.18
  117.7 80.9 %reduce-scatter.13.cloned.1.call-done = f32[64,128]{1,0:T(8,128)} async-done(((f32[1024,128]{1,0:T(8,128)}), f32[64,128]{1,0:T(8,128)}) %reduce-scatter.13.cloned.1.call-update) | async-done | bytes 32784
  199.7 21.7 %all_gather.17 = f32[1024,64]{1,0:T(8,128)S(1)} all-gather(f32[64,64]{1,0:T(8,128)S(1)} %copy.12), channel_id=1, replica_groups=mesh['cell'=32,'gene'=16] {'gene'}, dimensions={0}, use_global_device_ids=true | all-gather | bytes 278528 | tf_op jit(solution)/shard_map/all_gather | solution.py:57
  221.4 3.5 fusion.41
  225.0 3.6 fusion.13
  228.6 4.0 fusion.4
  232.6 1.0 copy.20
  233.7 134.7 %reduce-scatter.15.cloned.1.call-done = f32[32,128]{1,0:T(8,128)} async-done(((f32[1024,128]{1,0:T(8,128)}), f32[32,128]{1,0:T(8,128)}) %reduce-scatter.15.cloned.1.call-update) | async-done | bytes 16400
  369.5 61.9 %all_gather.18 = f32[1024,64]{1,0:T(8,128)S(1)} all-gather(f32[32,64]{1,0:T(8,128)S(1)} %copy.14), channel_id=1, replica_groups=mesh['cell'=32,'gene'=16] {'cell'}, dimensions={0}, use_global_device_ids=true | all-gather | bytes 270336 | tf_op jit(solution)/shard_map/all_gather | solution.py:80
  431.5 3.6 fusion.42
  435.0 4.9 fusion.14
  440.0 5.3 fusion.2
  445.3 1.0 copy.22
  446.4 88.3 %reduce-scatter.17.cloned.1.call-done = f32[64,128]{1,0:T(8,128)} async-done(((f32[1024,128]{1,0:T(8,128)}), f32[64,128]{1,0:T(8,128)}) %reduce-scatter.17.cloned.1.call-update) | async-done | bytes 32784
  535.9 21.4 %all_gather.19 = f32[1024,64]{1,0:T(8,128)S(1)} all-gather(f32[64,64]{1,0:T(8,128)S(1)} %copy.16), channel_id=1, replica_groups=mesh['cell'=32,'gene'=16] {'gene'}, dimensions={0}, use_global_device_ids=true | all-gather | bytes 278528 | tf_op jit(solution)/shard_map/all_gather | solution.py:57
  557.3 3.6 fusion.43
  560.8 3.6 fusion.15
  564.4 4.0 fusion
  569.5 134.7 %reduce-scatter.19.cloned.1.call-done = f32[32,128]{1,0:T(8,128)} async-done(((f32[1024,128]{1,0:T(8,128)}), f32[32,128]{1,0:T(8,128)}) %reduce-scatter.19.cloned.1.call-update) | async-done | bytes 16400
  (53 shorter events, 6.8 us)
Async XLA Ops:
  7.2 99.1 %copy-start.4 = (f32[1024]{0:T(1024)S(1)}, f32[1024]{0:T(1024)}, u32[]{:S(2)}) copy-start(f32[1024]{0:T(1024)} %param.9) | copy-start | bytes 12292
  7.2 99.1 %copy-start.5 = (f32[1024]{0:T(1024)S(1)}, f32[1024]{0:T(1024)}, u32[]{:S(2)}) copy-start(f32[1024]{0:T(1024)} %param.8) | copy-start | bytes 12292
  7.2 191.4 %reduce-scatter.13.cloned.1.call-start = ((), (), s32[]{:S(2)}) async-start(), calls=%async_computation.4 | async-start | bytes 557056
  102.7 8.5 %copy-start = (s32[1024,1024]{1,0:T(8,128)S(1)}, s32[1024,1024]{1,0:T(8,128)}, u32[]{:S(2)}) copy-start(s32[1024,1024]{1,0:T(8,128)} %param.5) | copy-start | bytes 12582916
  111.2 6.4 copy-start.6
  117.6 250.9 %reduce-scatter.15.cloned.1.call-start = ((), (), s32[]{:S(2)}) async-start(), calls=%async_computation.5 | async-start | bytes 540672
  221.4 7.1 %copy-start.1 = (s32[1024,1024]{1,0:T(8,128)S(1)}, s32[1024,1024]{1,0:T(8,128)}, u32[]{:S(2)}) copy-start(s32[1024,1024]{1,0:T(8,128)} %param.5) | copy-start | bytes 12582916
  228.5 5.1 copy-start.8
  233.6 301.1 %reduce-scatter.17.cloned.1.call-start = ((), (), s32[]{:S(2)}) async-start(), calls=%async_computation.6 | async-start | bytes 557056
  431.5 8.5 %copy-start.2 = (s32[1024,1024]{1,0:T(8,128)S(1)}, s32[1024,1024]{1,0:T(8,128)}, u32[]{:S(2)}) copy-start(s32[1024,1024]{1,0:T(8,128)} %param.5) | copy-start | bytes 12582916
  446.3 257.8 %reduce-scatter.19.cloned.1.call-start = ((), (), s32[]{:S(2)}) async-start(), calls=%async_computation.7 | async-start | bytes 540672
  535.8 28.6 %copy-start.7 = (f32[64,64]{1,0:T(8,128)}, f32[64,64]{1,0:T(8,128)S(1)}, u32[]{:S(2)}) copy-start(f32[64,64]{1,0:T(8,128)S(1)} %copy.16) | copy-start | bytes 49156
  557.3 7.1 %copy-start.3 = (s32[1024,1024]{1,0:T(8,128)S(1)}, s32[1024,1024]{1,0:T(8,128)}, u32[]{:S(2)}) copy-start(s32[1024,1024]{1,0:T(8,128)} %param.5) | copy-start | bytes 12582916
Sparse Core Ops, SparseCore 0:
  117.7 80.8 reduce-scatter.12
  233.7 134.6 reduce-scatter.14
  446.4 88.1 reduce-scatter.16
  569.6 134.5 reduce-scatter.18
where the time goes:
time: 722 us; the launch traced here: 713 us
  waiting for transfers between devices  439 us (61%)
  blocking collectives  201 us (28%)
  matrix products  49.6 us (7%)
  between operations  14.2 us (2%)
  local copies, waits for them, and re-layouts  9.25 us (1%)
    unnamed x8, waiting for transfers between devices  439 us
    all_gather x1, blocking collectives, per_device(): loading_block = lax.all_gather(loadings, 'cell', axis=0, tiled=True)  72.5 us
    all_gather x1, blocking collectives, per_device(): loading_block = lax.all_gather(own_v, 'cell', axis=0, tiled=True)  61.9 us
    all_gather x2, blocking collectives, per_device(): factor_block = lax.all_gather(own_u, 'gene', axis=0, tiled=True)  43.1 us
    all_gather x1, blocking collectives, per_device(): factor_block = lax.all_gather(factors, 'gene', axis=0, tiled=True)  23 us
  transfers between devices with their start and end apart: 4, of which 4 were waited for; matrix products, arithmetic and copies ran while one was open for 0% of the time, Pallas kernels for 0%

commit v1 on v0

v1 whole, which is shorter than its diff:
```python
import functools

import jax
import jax.numpy as jnp
from jax import lax
from jax.experimental import pallas as pl
from jax.experimental.pallas import tpu as pltpu
from jax.sharding import PartitionSpec as P

ITERS = 2
EPSILON = 1e-06
STEP_CAP = 0.25
LOG2E = 1.4426950408889634
F32, BF16 = jnp.float32, jnp.bfloat16
MESH = pl.DeviceIdType.MESH

ZG, ZL, YL = 4, 4, 2
X, YH, CO = 4, 2, 2
RANK = 64
UROWS, VROWS = 64, 32
CELLS = X * YH * CO * UROWS
GENES = ZG * ZL * YL * VROWS
UCHUNK = YH * CO * UROWS
VCHUNK = ZL * YL * VROWS
FAR_FIRST = (2, 1, 3, 0)
U_CORE = 0
U_CHIP = U_CORE + X
V_PAIR = U_CHIP + X * YH
V_LINE = V_PAIR + ZG
V_RING = V_LINE + ZG * ZL
GU_CHIP = V_RING + ZG
GU_CORE = GU_CHIP + X * YH
GV_RING = GU_CORE + X * YH
GV_LINE = GV_RING + ZG
GV_PAIR = GV_LINE + ZG * ZL
SLOTS = GV_PAIR + ZG


def split(x):
    high = x.astype(BF16).astype(F32)
    return high, x - high


def left_half(shape):
    return lax.broadcasted_iota(jnp.int32, shape, len(shape) - 1) < RANK


def swap(x):
    return pltpu.roll(x, RANK, axis=x.ndim - 1)


def pairs(left, right):
    mask = left_half(left.shape)
    first = jnp.where(mask, left, swap(right))
    second = jnp.where(mask, swap(left), right)
    return first, second


def unpack_to(ref, column, block, left, right):
    first, second = pairs(left, right)
    n = first.shape[-2]
    ref[pl.ds(block, n), pl.ds(column, 128)] = first.astype(BF16)
    ref[pl.ds(block + n, n), pl.ds(column, 128)] = second.astype(BF16)


def far_first(j):
    return (2 + 3 * j - (j * (j - 1)) // 2) % 4


def kernel(
    counts_hbm, u_ref, v_ref, cell_ref, gene_ref, new_u, new_v,
    cnt32, cnt, cnt_t, u_eta, u_sum, v_eta, v_sum, cell_cols, gene_cols,
    own_u, own_v, ubuf, vbuf, part_u, core_in, sum_u, chip_in,
    part_v, pair_in, sum1, line_in, sum2, ring_in, load_sem, send_sem, recv_sem,
):
    c, g = lax.axis_index("cell"), lax.axis_index("gene")
    z, yl = c // YL, c % YL
    zg, zl = z // ZL, z % ZL
    chip, co = g // CO, g % CO
    x, yh = chip // YH, chip % YH

    def cell_dev(dg, dl, dy):
        there = ((zg + dg) % ZG) * ZL + (zl + dl) % ZL
        return (there * YL + (yl + dy) % YL, g)

    def gene_dev(dx, dh, dc):
        there = ((x + dx) % X) * YH + (yh + dh) % YH
        return (c, there * CO + (co + dc) % CO)

    chips = [(dx, dh) for dx in FAR_FIRST for dh in (1, 0) if dx or dh]
    peers = [gene_dev(dx, dh, 0) for dx, dh in chips] + [gene_dev(0, 0, 1)]
    peers += [cell_dev(d, 0, 0) for d in (2, 1, 3)]
    peers += [cell_dev(0, d, 0) for d in (1, 2, 3)] + [cell_dev(0, 0, 1)]
    barrier = pltpu.get_barrier_semaphore()
    for peer in peers:
        pl.semaphore_signal(barrier, inc=1, device_id=peer, device_id_type=MESH)

    def load(k):
        rows = pl.ds(k * 256, 256)
        return pltpu.make_async_copy(counts_hbm.at[rows], cnt32.at[rows], load_sem.at[k])

    for k in range(CELLS // 256):
        load(k).start()

    started = []

    def send(era, slot, src, dst, device):
        copy = pltpu.make_async_remote_copy(
            src_ref=src, dst_ref=dst, send_sem=send_sem.at[era, slot],
            recv_sem=recv_sem.at[era, slot], device_id=device, device_id_type=MESH,
        )
        copy.start()

    def sent(era, slot, src, dst, device):
        send(era, slot, src, dst, device)
        started.append((era, slot, src))

    def arrived(era, slot, ref):
        pltpu.make_async_remote_copy(
            src_ref=ref, dst_ref=ref, send_sem=send_sem.at[era, slot],
            recv_sem=recv_sem.at[era, slot], device_id=(c, g), device_id_type=MESH,
        ).wait_recv()

    def pack(rows):
        half = rows.shape[0] // 2
        return jnp.where(left_half((half, 128)), rows[:half], swap(rows[half:]))

    own_u[...] = jnp.zeros_like(own_u)
    own_v[...] = jnp.zeros_like(own_v)
    own_u[:, :RANK] = u_ref[...]
    own_v[:, :RANK] = v_ref[...]

    def offset_columns(row, first_offset, first_one, out):
        high, rest = split(row)
        mid, low = split(rest)
        index = lax.broadcasted_iota(jnp.int32, (128, row.shape[1]), 0)
        rows = jnp.zeros((128, row.shape[1]), F32)
        for k, part in enumerate((high, mid, low)):
            rows = jnp.where(index == first_offset + k, part, rows)
            rows = jnp.where(index == first_one + k, 1.0, rows)
        out[...] = rows.T

    ubuf[0, chip, co] = pack(own_u[...])
    vbuf[0, zg, zl, yl] = pack(own_v[...])
    pl.semaphore_wait(barrier, len(peers))

    def gather_u_start(era):
        mine = ubuf.at[era, chip, co]
        for dx, dh in chips:
            sent(era, GU_CHIP + dx * YH + dh, mine, mine, gene_dev(dx, dh, 0))
        sent(era, GU_CORE, mine, mine, gene_dev(0, 0, 1))

    def gather_u_finish(era):
        order = [(1, 0), (3, 0), (0, 1), (2, 0), (1, 1), (3, 1), (2, 1)]
        for dx, dh in order:
            block = ubuf.at[era, ((x - dx) % X) * YH + (yh - dh) % YH, co]
            arrived(era, GU_CHIP + dx * YH + dh, block)
            sent(era, GU_CORE + dx * YH + dh, block, block, gene_dev(0, 0, 1))
        for dx, dh in [(0, 0)] + order:
            block = ubuf.at[era, ((x - dx) % X) * YH + (yh - dh) % YH, 1 - co]
            arrived(era, GU_CORE + dx * YH + dh, block)

    def v_line(era, e):
        block = vbuf.at[era, (zg - e) % ZG, zl, yl]
        for d in (3, 2, 1):
            sent(era, GV_LINE + e * ZL + d, block, block, cell_dev(0, d, 0))

    def v_pair(era, e):
        for d in (1, 2, 3):
            arrived(era, GV_LINE + e * ZL + d, vbuf.at[era, (zg - e) % ZG, (zl - d) % ZL, yl])
        blocks = vbuf.at[era, (zg - e) % ZG, :, yl]
        sent(era, GV_PAIR + e, blocks, blocks, cell_dev(0, 0, 1))

    def v_ring(era, e):
        arrived(era, GV_RING + e, vbuf.at[era, (zg - e) % ZG, zl, yl])
        v_line(era, e)

    def gather_v_start(era):
        mine = vbuf.at[era, zg, zl, yl]
        for d in (2, 1, 3):
            sent(era, GV_RING + d, mine, mine, cell_dev(d, 0, 0))
        v_line(era, 0)

    def gather_v_finish(era):
        v_pair(era, 0)
        v_ring(era, 1)
        v_ring(era, 3)
        v_pair(era, 1)
        v_pair(era, 3)
        v_ring(era, 2)
        v_pair(era, 2)
        for e in (0, 1, 3, 2):
            arrived(era, GV_PAIR + e, vbuf.at[era, (zg - e) % ZG, :, 1 - yl])

    def assemble(packed, rows, eta, total, columns, scale):
        plain_h, plain_l = split(packed)
        square_h, square_l = split(packed * packed)
        n = rows // 2

        def put(ref, column, left, right):
            first, second = pairs(left, right)
            both = jnp.concatenate([first.astype(BF16), second.astype(BF16)], axis=1)
            ref[:, column:column + 128] = both.reshape(ref.shape[0], 128)

        put(total, 0, plain_h, square_h)
        put(total, 128, plain_l, square_l)
        mask = left_half(columns.shape)
        if scale:
            high, low = split(packed * LOG2E)
            put(eta, 0, high, low)
            third = high
        else:
            put(eta, 0, plain_h, plain_h)
            third = plain_l
        first, second = pairs(third, third)
        both = jnp.concatenate([first, second], axis=1).reshape(eta.shape[0], 128)
        eta[:, 128:] = jnp.where(mask, both, columns[...]).astype(BF16)

    def assemble_u(era):
        assemble(ubuf[era].reshape(X * YH * CO, UROWS // 2, 128), UROWS, u_eta, u_sum, cell_cols, True)

    def assemble_v(era):
        assemble(vbuf[era].reshape(ZG * ZL * YL, VROWS // 2, 128), VROWS, v_eta, v_sum, gene_cols, False)

    def sums(row_eta, column_eta, weights, count_ref, first, rows):
        here = pl.ds(pl.multiple_of(first, rows), rows)
        eta = lax.dot_general(
            row_eta[here, :], column_eta[...], (((1,), (1,)), ((), ())), preferred_element_type=F32
        )
        means = jnp.exp2(eta)
        high = means.astype(BF16)
        low = (means - high.astype(F32)).astype(BF16)
        w = weights[...]
        acc = jnp.dot(high, w, preferred_element_type=F32) + jnp.dot(low, w, preferred_element_type=F32)
        seen = jnp.dot(count_ref[here, :], w, preferred_element_type=F32)
        total = acc[:, :128] + acc[:, 128:]
        seen = seen[:, :128] + seen[:, 128:]
        return total - jnp.where(left_half(seen.shape), seen, 0.0)

    def updated(own, total):
        return own - STEP_CAP * jnp.tanh((total / (swap(total) + EPSILON)) / STEP_CAP)

    def factor_step(it):
        def chunk(j, carry):
            there = (x + far_first(j)) % X
            out = sums(u_eta, v_eta, v_sum, cnt, there * UCHUNK, UCHUNK)
            part_u[it, there] = out.reshape(YH, CO, UROWS, 128)
            send(it, U_CORE + j, part_u.at[it, there, :, 1 - co], core_in.at[it, j], gene_dev(0, 0, 1))
            return carry

        lax.fori_loop(0, X, chunk, 0)
        for j, dx in enumerate(FAR_FIRST):
            there = (x + dx) % X
            started.append((it, U_CORE + j, core_in.at[it, j]))
            arrived(it, U_CORE + j, core_in.at[it, j])
            sum_u[it, j] = part_u[it, there, :, co] + core_in[it, j]
            for dh in (1, 0):
                if dx or dh:
                    slot = dx * YH + dh
                    sent(it, U_CHIP + slot, sum_u.at[it, j, (yh + dh) % YH], chip_in.at[it, slot], gene_dev(dx, dh, 0))
        total = sum_u[it, len(FAR_FIRST) - 1, yh]
        for dx, dh in [(1, 0), (3, 0), (0, 1), (2, 0), (1, 1), (3, 1), (2, 1)]:
            slot = dx * YH + dh
            arrived(it, U_CHIP + slot, chip_in.at[it, slot])
            total = total + chip_in[it, slot]
        own_u[...] = updated(own_u[...], total)

    def loading_step(it):
        def chunk(j, carry):
            there = (zg + far_first(j)) % ZG
            out = sums(v_eta, u_eta, u_sum, cnt_t, there * VCHUNK, VCHUNK)
            part_v[it, there] = out.reshape(ZL, YL, VROWS, 128)
            send(it, V_PAIR + j, part_v.at[it, there, :, 1 - yl], pair_in.at[it, j], cell_dev(0, 0, 1))
            return carry

        lax.fori_loop(0, ZG, chunk, 0)
        for j, dg in enumerate(FAR_FIRST):
            there = (zg + dg) % ZG
            started.append((it, V_PAIR + j, pair_in.at[it, j]))
            arrived(it, V_PAIR + j, pair_in.at[it, j])
            sum1[it, j] = part_v[it, there, :, yl] + pair_in[it, j]
            for d in (3, 2, 1):
                sent(it, V_LINE + j * ZL + d, sum1.at[it, j, (zl + d) % ZL], line_in.at[it, j, d], cell_dev(0, d, 0))
        for j, dg in enumerate(FAR_FIRST):
            total = sum1[it, j, zl]
            for d in (1, 2, 3):
                arrived(it, V_LINE + j * ZL + d, line_in.at[it, j, d])
                total = total + line_in[it, j, d]
            if dg:
                sum2[it, j] = total
                sent(it, V_RING + dg, sum2.at[it, j], ring_in.at[it, dg], cell_dev(dg, 0, 0))
        for dg in (1, 3, 2):
            arrived(it, V_RING + dg, ring_in.at[it, dg])
            total = total + ring_in[it, dg]
        own_v[...] = updated(own_v[...], total)

    gather_v_start(0)
    gather_u_start(0)
    offset_columns(cell_ref[...] * LOG2E, RANK, RANK + 3, cell_cols)
    offset_columns(gene_ref[...] * LOG2E, RANK + 3, RANK, gene_cols)

    def prepare(k, carry):
        load(k).wait()
        rows = pl.ds(pl.multiple_of(k * 256, 256), 256)
        block = cnt32[rows, :].astype(F32)
        cnt[rows, :] = block.astype(BF16)
        cnt_t[:, rows] = block.T.astype(BF16)
        return carry

    gather_u_finish(0)
    lax.fori_loop(0, CELLS // 256, prepare, 0)
    gather_v_finish(0)
    assemble_u(0)
    assemble_v(0)
    for it in range(ITERS):
        factor_step(it)
        ubuf[it + 1, chip, co] = pack(own_u[...])
        if it + 1 == ITERS:
            new_u[...] = own_u[:, :RANK]
        gather_u_start(it + 1)
        gather_u_finish(it + 1)
        assemble_u(it + 1)
        loading_step(it)
        if it + 1 < ITERS:
            vbuf[it + 1, zg, zl, yl] = pack(own_v[...])
            gather_v_start(it + 1)
            gather_v_finish(it + 1)
            assemble_v(it + 1)
    new_v[...] = own_v[:, :RANK]
    for era, slot, src in started:
        pltpu.make_async_remote_copy(
            src_ref=src, dst_ref=src, send_sem=send_sem.at[era, slot],
            recv_sem=recv_sem.at[era, slot], device_id=(c, g), device_id_type=MESH,
        ).wait_send()


def per_device(counts, factors, loadings, cell_offset, gene_offset):
    vmem = pl.BlockSpec(memory_space=pltpu.VMEM)
    scratch = [
        pltpu.VMEM((CELLS, GENES), jnp.int32),
        pltpu.VMEM((CELLS, GENES), BF16),
        pltpu.VMEM((GENES, CELLS), BF16),
        pltpu.VMEM((CELLS, 256), BF16),
        pltpu.VMEM((CELLS, 256), BF16),
        pltpu.VMEM((GENES, 256), BF16),
        pltpu.VMEM((GENES, 256), BF16),
        pltpu.VMEM((CELLS, 128), F32),
        pltpu.VMEM((GENES, 128), F32),
        pltpu.VMEM((UROWS, 128), F32),
        pltpu.VMEM((VROWS, 128), F32),
        pltpu.VMEM((ITERS + 1, X * YH, CO, UROWS // 2, 128), F32),
        pltpu.VMEM((ITERS, ZG, ZL, YL, VROWS // 2, 128), F32),
        pltpu.VMEM((ITERS, X, YH, CO, UROWS, 128), F32),
        pltpu.VMEM((ITERS, X, YH, UROWS, 128), F32),
        pltpu.VMEM((ITERS, X, YH, UROWS, 128), F32),
        pltpu.VMEM((ITERS, X * YH, UROWS, 128), F32),
        pltpu.VMEM((ITERS, ZG, ZL, YL, VROWS, 128), F32),
        pltpu.VMEM((ITERS, ZG, ZL, VROWS, 128), F32),
        pltpu.VMEM((ITERS, ZG, ZL, VROWS, 128), F32),
        pltpu.VMEM((ITERS, ZG, ZL, VROWS, 128), F32),
        pltpu.VMEM((ITERS, ZG, VROWS, 128), F32),
        pltpu.VMEM((ITERS, ZG, VROWS, 128), F32),
        pltpu.SemaphoreType.DMA((CELLS // 256,)),
        pltpu.SemaphoreType.DMA((ITERS + 1, SLOTS)),
        pltpu.SemaphoreType.DMA((ITERS + 1, SLOTS)),
    ]
    return pl.pallas_call(
        kernel,
        name="sweeps",
        out_shape=(
            jax.ShapeDtypeStruct((UROWS, RANK), F32),
            jax.ShapeDtypeStruct((VROWS, RANK), F32),
        ),
        in_specs=[pl.BlockSpec(memory_space=pl.ANY), vmem, vmem, vmem, vmem],
        out_specs=(vmem, vmem),
        scratch_shapes=scratch,
        compiler_params=pltpu.CompilerParams(
            collective_id=0, has_side_effects=True, vmem_limit_bytes=48 * 1024 * 1024
        ),
    )(counts, factors, loadings, cell_offset.reshape(1, -1), gene_offset.reshape(1, -1))


def solution(mesh):
    in_specs = (
        P("cell", "gene"),
        P(("cell", "gene"), None),
        P(("gene", "cell"), None),
        P("cell"),
        P("gene"),
    )
    out_specs = (P(("cell", "gene"), None), P(("gene", "cell"), None))
    return jax.shard_map(
        per_device, mesh=mesh, in_specs=in_specs, out_specs=out_specs, check_vma=False
    )
```

time: 722 us -> 126 us (0.17)
  the two profiles are of different devices: /device:TPU:2 before, /device:TPU:1 now
where the time goes in v1:
time: 126 us; the launch traced here: 125 us
  Pallas kernels  119 us (94%)
  local copies, waits for them, and re-layouts  6.25 us (5%)
    pallas_call x1, Pallas kernels, per_device(): pl.pallas_call(kernel, name='sweeps', out_shape=(jax.ShapeDtypeStruct((UR...  119 us
    unnamed x12, local copies, waits for them, and re-layouts  6.25 us

profile of v1, /device:TPU:1, one launch (start us, length us, event | category | flops | bytes accessed | tf_op | source)
XLA Modules:
  0.0 125.5 jit_solution(2178358816547159804)
XLA Ops:
  0.6 0.0 copy-start
  0.6 2.2 %copy-done = s32[1024,1024]{1,0:T(8,128)S(1)} copy-done((s32[1024,1024]{1,0:T(8,128)S(1)}, s32[1024,1024]{1,0:T(8,128)}, u32[]{:S(2)}) %copy-start) | copy-done | bytes 4194328
  2.8 0.0 copy-start.1
  2.8 0.8 copy-done.1
  3.6 0.0 copy-start.2
  3.6 0.7 copy-done.2
  4.3 0.0 copy-start.3
  4.3 0.7 copy-done.3
  5.0 0.0 copy-start.4
  5.0 0.7 copy-done.4
  5.7 118.6 %sweeps.1 = (f32[64,64]{1,0:T(8,128)S(1)}, f32[32,64]{1,0:T(8,128)S(1)}) custom-call(s32[1024,1024]{1,0:T(8,128)S(1)} %copy-done, f32[64,64]{1,0:T(8,128)S(1)} %copy-done.1, f32[32,64]{1,0:T(8,128)S(1)} %copy-done.2, f32[1,1024]{1,0:T(1,128)S(1)} %bitcast.2, f32[1,1024]{1,0:T(1,128)S(1)} %bitcast.3), custom_call_target="tpu_custom_call" | custom-call | tf_op jit(solution)/shard_map/sweeps/pallas_call | solution.py:367
  124.3 0.6 copy.9
  124.9 0.6 copy.10
Async XLA Ops:
  0.6 2.2 %copy-start = (s32[1024,1024]{1,0:T(8,128)S(1)}, s32[1024,1024]{1,0:T(8,128)}, u32[]{:S(2)}) copy-start(s32[1024,1024]{1,0:T(8,128)} %counts_hbm.1) | copy-start | bytes 12582916
  2.8 0.8 copy-start.1
  3.6 0.7 copy-start.2
  4.3 0.7 copy-start.3
  5.0 0.7 copy-start.4

commit v2 on v1

--- a/solution.py
+++ b/solution.py
@@ -15,6 +15,7 @@
 MESH = pl.DeviceIdType.MESH
 
 ZG, ZL, YL = 4, 4, 2
+Z = ZG * ZL
 X, YH, CO = 4, 2, 2
 RANK = 64
 UROWS, VROWS = 64, 32
@@ -30,10 +31,9 @@
 V_RING = V_LINE + ZG * ZL
 GU_CHIP = V_RING + ZG
 GU_CORE = GU_CHIP + X * YH
-GV_RING = GU_CORE + X * YH
-GV_LINE = GV_RING + ZG
-GV_PAIR = GV_LINE + ZG * ZL
-SLOTS = GV_PAIR + ZG
+GV_Z = GU_CORE + X * YH
+GV_PAIR = GV_Z + ZG * ZL
+SLOTS = GV_PAIR + ZG * ZL
 
 
 def split(x):
@@ -68,8 +68,8 @@
 
 
 def kernel(
-    counts_hbm, u_ref, v_ref, cell_ref, gene_ref, new_u, new_v,
-    cnt32, cnt, cnt_t, u_eta, u_sum, v_eta, v_sum, cell_cols, gene_cols,
+    counts_hbm, u_hbm, v_hbm, cell_hbm, gene_hbm, new_rows,
+    u_ref, v_ref, cell_ref, gene_ref, cnt32, cnt, cnt_t, u_eta, u_sum, v_eta, v_sum, cell_cols, gene_cols,
     own_u, own_v, ubuf, vbuf, part_u, core_in, sum_u, chip_in,
     part_v, pair_in, sum1, line_in, sum2, ring_in, load_sem, send_sem, recv_sem,
 ):
@@ -87,10 +87,13 @@
         there = ((x + dx) % X) * YH + (yh + dh) % YH
         return (c, there * CO + (co + dc) % CO)
 
+    def z_dev(d):
+        return (((z + d) % Z) * YL + yl, g)
+
+    far = [d for k in range(Z // 2, 0, -1) for d in dict.fromkeys((k, Z - k))]
     chips = [(dx, dh) for dx in FAR_FIRST for dh in (1, 0) if dx or dh]
-    peers = [gene_dev(dx, dh, 0) for dx, dh in chips] + [gene_dev(0, 0, 1)]
-    peers += [cell_dev(d, 0, 0) for d in (2, 1, 3)]
-    peers += [cell_dev(0, d, 0) for d in (1, 2, 3)] + [cell_dev(0, 0, 1)]
+    peers = [z_dev(d) for d in far] + [gene_dev(dx, dh, 0) for dx, dh in chips]
+    peers += [cell_dev(0, 0, 1), gene_dev(0, 0, 1)]
     barrier = pltpu.get_barrier_semaphore()
     for peer in peers:
         pl.semaphore_signal(barrier, inc=1, device_id=peer, device_id_type=MESH)
@@ -99,6 +102,14 @@
         rows = pl.ds(k * 256, 256)
         return pltpu.make_async_copy(counts_hbm.at[rows], cnt32.at[rows], load_sem.at[k])
 
+    small = [
+        pltpu.make_async_copy(src, dst, load_sem.at[CELLS // 256 + k])
+        for k, (src, dst) in enumerate(
+            ((v_hbm, v_ref), (u_hbm, u_ref), (cell_hbm, cell_ref), (gene_hbm, gene_ref))
+        )
+    ]
+    for copy in small:
+        copy.start()
     for k in range(CELLS // 256):
         load(k).start()
 
@@ -127,6 +138,8 @@
 
     own_u[...] = jnp.zeros_like(own_u)
     own_v[...] = jnp.zeros_like(own_v)
+    for copy in small:
+        copy.wait()
     own_u[:, :RANK] = u_ref[...]
     own_v[:, :RANK] = v_ref[...]
 
@@ -141,7 +154,7 @@
         out[...] = rows.T
 
     ubuf[0, chip, co] = pack(own_u[...])
-    vbuf[0, zg, zl, yl] = pack(own_v[...])
+    vbuf[0, z, yl] = pack(own_v[...])
     pl.semaphore_wait(barrier, len(peers))
 
     def gather_u_start(era):
@@ -160,37 +173,20 @@
             block = ubuf.at[era, ((x - dx) % X) * YH + (yh - dh) % YH, 1 - co]
             arrived(era, GU_CORE + dx * YH + dh, block)
 
-    def v_line(era, e):
-        block = vbuf.at[era, (zg - e) % ZG, zl, yl]
-        for d in (3, 2, 1):
-            sent(era, GV_LINE + e * ZL + d, block, block, cell_dev(0, d, 0))
-
-    def v_pair(era, e):
-        for d in (1, 2, 3):
-            arrived(era, GV_LINE + e * ZL + d, vbuf.at[era, (zg - e) % ZG, (zl - d) % ZL, yl])
-        blocks = vbuf.at[era, (zg - e) % ZG, :, yl]
-        sent(era, GV_PAIR + e, blocks, blocks, cell_dev(0, 0, 1))
-
-    def v_ring(era, e):
-        arrived(era, GV_RING + e, vbuf.at[era, (zg - e) % ZG, zl, yl])
-        v_line(era, e)
-
     def gather_v_start(era):
-        mine = vbuf.at[era, zg, zl, yl]
-        for d in (2, 1, 3):
-            sent(era, GV_RING + d, mine, mine, cell_dev(d, 0, 0))
-        v_line(era, 0)
+        mine = vbuf.at[era, z, yl]
+        for d in far:
+            sent(era, GV_Z + d, mine, mine, z_dev(d))
+        sent(era, GV_PAIR, mine, mine, cell_dev(0, 0, 1))
 
     def gather_v_finish(era):
-        v_pair(era, 0)
-        v_ring(era, 1)
-        v_ring(era, 3)
-        v_pair(era, 1)
-        v_pair(era, 3)
-        v_ring(era, 2)
-        v_pair(era, 2)
-        for e in (0, 1, 3, 2):
-            arrived(era, GV_PAIR + e, vbuf.at[era, (zg - e) % ZG, :, 1 - yl])
+        near = [d for d in reversed(far)]
+        for d in near:
+            block = vbuf.at[era, (z - d) % Z, yl]
+            arrived(era, GV_Z + d, block)
+            sent(era, GV_PAIR + d, block, block, cell_dev(0, 0, 1))
+        for d in [0] + near:
+            arrived(era, GV_PAIR + d, vbuf.at[era, (z - d) % Z, 1 - yl])
 
     def assemble(packed, rows, eta, total, columns, scale):
         plain_h, plain_l = split(packed)
@@ -316,17 +312,17 @@
         factor_step(it)
         ubuf[it + 1, chip, co] = pack(own_u[...])
         if it + 1 == ITERS:
-            new_u[...] = own_u[:, :RANK]
+            new_rows[:UROWS] = own_u[...]
         gather_u_start(it + 1)
         gather_u_finish(it + 1)
         assemble_u(it + 1)
         loading_step(it)
         if it + 1 < ITERS:
-            vbuf[it + 1, zg, zl, yl] = pack(own_v[...])
+            vbuf[it + 1, z, yl] = pack(own_v[...])
             gather_v_start(it + 1)
             gather_v_finish(it + 1)
             assemble_v(it + 1)
-    new_v[...] = own_v[:, :RANK]
+    new_rows[UROWS:] = own_v[...]
     for era, slot, src in started:
         pltpu.make_async_remote_copy(
             src_ref=src, dst_ref=src, send_sem=send_sem.at[era, slot],
@@ -336,7 +332,12 @@
 
 def per_device(counts, factors, loadings, cell_offset, gene_offset):
     vmem = pl.BlockSpec(memory_space=pltpu.VMEM)
+    hbm = pl.BlockSpec(memory_space=pltpu.HBM)
     scratch = [
+        pltpu.VMEM((UROWS, RANK), F32),
+        pltpu.VMEM((VROWS, RANK), F32),
+        pltpu.VMEM((1, CELLS), F32),
+        pltpu.VMEM((1, GENES), F32),
         pltpu.VMEM((CELLS, GENES), jnp.int32),
         pltpu.VMEM((CELLS, GENES), BF16),
         pltpu.VMEM((GENES, CELLS), BF16),
@@ -349,7 +350,7 @@
         pltpu.VMEM((UROWS, 128), F32),
         pltpu.VMEM((VROWS, 128), F32),
         pltpu.VMEM((ITERS + 1, X * YH, CO, UROWS // 2, 128), F32),
-        pltpu.VMEM((ITERS, ZG, ZL, YL, VROWS // 2, 128), F32),
+        pltpu.VMEM((ITERS, Z, YL, VROWS // 2, 128), F32),
         pltpu.VMEM((ITERS, X, YH, CO, UROWS, 128), F32),
         pltpu.VMEM((ITERS, X, YH, UROWS, 128), F32),
         pltpu.VMEM((ITERS, X, YH, UROWS, 128), F32),
@@ -360,24 +361,22 @@
         pltpu.VMEM((ITERS, ZG, ZL, VROWS, 128), F32),
         pltpu.VMEM((ITERS, ZG, VROWS, 128), F32),
         pltpu.VMEM((ITERS, ZG, VROWS, 128), F32),
-        pltpu.SemaphoreType.DMA((CELLS // 256,)),
+        pltpu.SemaphoreType.DMA((CELLS // 256 + 4,)),
         pltpu.SemaphoreType.DMA((ITERS + 1, SLOTS)),
         pltpu.SemaphoreType.DMA((ITERS + 1, SLOTS)),
     ]
-    return pl.pallas_call(
+    rows = pl.pallas_call(
         kernel,
         name="sweeps",
-        out_shape=(
-            jax.ShapeDtypeStruct((UROWS, RANK), F32),
-            jax.ShapeDtypeStruct((VROWS, RANK), F32),
-        ),
-        in_specs=[pl.BlockSpec(memory_space=pl.ANY), vmem, vmem, vmem, vmem],
-        out_specs=(vmem, vmem),
+        out_shape=jax.ShapeDtypeStruct((UROWS + VROWS, 128), F32),
+        in_specs=[hbm] * 5,
+        out_specs=vmem,
         scratch_shapes=scratch,
         compiler_params=pltpu.CompilerParams(
-            collective_id=0, has_side_effects=True, vmem_limit_bytes=48 * 1024 * 1024
+            collective_id=0, has_side_effects=True, vmem_limit_bytes=63 * 1024 * 1024
         ),
     )(counts, factors, loadings, cell_offset.reshape(1, -1), gene_offset.reshape(1, -1))
+    return rows[:UROWS, :RANK], rows[UROWS:, :RANK]
 
 
 def solution(mesh):

time: 126 us -> 115 us (0.913)
  Pallas kernels: 119 us -> 111 us
  local copies, waits for them, and re-layouts: 6.25 us -> 2.7 us
    pallas_call x1, Pallas kernels: 119 us -> 111 us  [per_device(): pl.pallas_call(kernel, name='sweeps', out_shape=jax.ShapeDtypeStruct((URO...]
    unnamed x12 -> x0, local copies, waits for them, and re-layouts: 6.25 us -> none
    slice x0 -> x2, local copies, waits for them, and re-layouts: none -> 2.7 us  [per_device(): return (rows[:UROWS, :RANK], rows[UROWS:, :RANK])]
where the time goes in v2:
time: 115 us; the launch traced here: 114 us
  Pallas kernels  111 us (97%)
  local copies, waits for them, and re-layouts  2.7 us (2%)
    pallas_call x1, Pallas kernels, per_device(): pl.pallas_call(kernel, name='sweeps', out_shape=jax.ShapeDtypeStruct((URO...  111 us
    slice x2, local copies, waits for them, and re-layouts, per_device(): return (rows[:UROWS, :RANK], rows[UROWS:, :RANK])  2.7 us

profile of v2, /device:TPU:1, one launch (start us, length us, event | category | flops | bytes accessed | tf_op | source)
XLA Modules:
  0.0 114.4 jit_solution(15641891581451041037)
XLA Ops:
  0.6 111.0 %sweeps.1 = f32[96,128]{1,0:T(8,128)} custom-call(s32[1024,1024]{1,0:T(8,128)} %counts_hbm.1, f32[64,64]{1,0:T(8,128)} %u_hbm.1, f32[32,64]{1,0:T(8,128)} %v_hbm.1, f32[1,1024]{1,0:T(1,128)} %bitcast.2, f32[1,1024]{1,0:T(1,128)} %bitcast.3), custom_call_target="tpu_custom_call" | custom-call | tf_op jit(solution)/shard_map/sweeps/pallas_call | solution.py:368
  111.7 1.3 %slice.7 = f32[32,64]{1,0:T(8,128)} slice(f32[96,128]{1,0:T(8,128)} %sweeps.1), slice={[64:96], [0:64]} | slice | bytes 16384 | tf_op jit(solution)/shard_map/slice | solution.py:379
  113.0 1.4 %slice.6 = f32[64,64]{1,0:T(8,128)} slice(f32[96,128]{1,0:T(8,128)} %sweeps.1), slice={[0:64], [0:64]} | slice | bytes 32768 | tf_op jit(solution)/shard_map/slice | solution.py:379

commit v3 on v2

--- a/solution.py
+++ b/solution.py
@@ -24,6 +24,9 @@
 UCHUNK = YH * CO * UROWS
 VCHUNK = ZL * YL * VROWS
 FAR_FIRST = (2, 1, 3, 0)
+ZROWS = YL * VROWS
+TILE = 256
+NEAR = 2
 U_CORE = 0
 U_CHIP = U_CORE + X
 V_PAIR = U_CHIP + X * YH
@@ -54,13 +57,6 @@
     first = jnp.where(mask, left, swap(right))
     second = jnp.where(mask, swap(left), right)
     return first, second
-
-
-def unpack_to(ref, column, block, left, right):
-    first, second = pairs(left, right)
-    n = first.shape[-2]
-    ref[pl.ds(block, n), pl.ds(column, 128)] = first.astype(BF16)
-    ref[pl.ds(block + n, n), pl.ds(column, 128)] = second.astype(BF16)
 
 
 def far_first(j):
@@ -143,7 +139,7 @@
     own_u[:, :RANK] = u_ref[...]
     own_v[:, :RANK] = v_ref[...]
 
-    def offset_columns(row, first_offset, first_one, out):
+    def offset_columns(row, first_offset, first_one, turn, out):
         high, rest = split(row)
         mid, low = split(rest)
         index = lax.broadcasted_iota(jnp.int32, (128, row.shape[1]), 0)
@@ -151,27 +147,32 @@
         for k, part in enumerate((high, mid, low)):
             rows = jnp.where(index == first_offset + k, part, rows)
             rows = jnp.where(index == first_one + k, 1.0, rows)
-        out[...] = rows.T
-
-    ubuf[0, chip, co] = pack(own_u[...])
+        out[...] = (rows if turn is None else pltpu.roll(rows, turn, axis=1)).T
+
+    ubuf[0, x, yh, co] = pack(own_u[...])
     vbuf[0, z, yl] = pack(own_v[...])
     pl.semaphore_wait(barrier, len(peers))
 
     def gather_u_start(era):
-        mine = ubuf.at[era, chip, co]
+        mine = ubuf.at[era, x, yh, co]
         for dx, dh in chips:
             sent(era, GU_CHIP + dx * YH + dh, mine, mine, gene_dev(dx, dh, 0))
         sent(era, GU_CORE, mine, mine, gene_dev(0, 0, 1))
 
-    def gather_u_finish(era):
-        order = [(1, 0), (3, 0), (0, 1), (2, 0), (1, 1), (3, 1), (2, 1)]
-        for dx, dh in order:
-            block = ubuf.at[era, ((x - dx) % X) * YH + (yh - dh) % YH, co]
+    def gather_u_forward(era):
+        for dx, dh in [(1, 0), (3, 0), (0, 1), (2, 0), (1, 1), (3, 1), (2, 1)]:
+            block = ubuf.at[era, (x - dx) % X, (yh - dh) % YH, co]
             arrived(era, GU_CHIP + dx * YH + dh, block)
             sent(era, GU_CORE + dx * YH + dh, block, block, gene_dev(0, 0, 1))
-        for dx, dh in [(0, 0)] + order:
-            block = ubuf.at[era, ((x - dx) % X) * YH + (yh - dh) % YH, 1 - co]
+
+    def factor_tile(era, dx):
+        for dh in range(YH):
+            block = ubuf.at[era, (x - dx) % X, (yh - dh) % YH, 1 - co]
             arrived(era, GU_CORE + dx * YH + dh, block)
+        there = (x - dx) % X
+        packed = ubuf[era, there].reshape(YH * CO, UROWS // 2, 128)
+        assemble(packed, there * TILE, u_eta, u_sum, cell_cols, True)
+        return there
 
     def gather_v_start(era):
         mine = vbuf.at[era, z, yl]
@@ -179,28 +180,31 @@
             sent(era, GV_Z + d, mine, mine, z_dev(d))
         sent(era, GV_PAIR, mine, mine, cell_dev(0, 0, 1))
 
-    def gather_v_finish(era):
-        near = [d for d in reversed(far)]
-        for d in near:
-            block = vbuf.at[era, (z - d) % Z, yl]
-            arrived(era, GV_Z + d, block)
-            sent(era, GV_PAIR + d, block, block, cell_dev(0, 0, 1))
-        for d in [0] + near:
-            arrived(era, GV_PAIR + d, vbuf.at[era, (z - d) % Z, 1 - yl])
-
-    def assemble(packed, rows, eta, total, columns, scale):
+    def gather_v_forward(era, first, last):
+        for d in reversed(far):
+            if first <= min(d, Z - d) <= last:
+                block = vbuf.at[era, (z - d) % Z, yl]
+                arrived(era, GV_Z + d, block)
+                sent(era, GV_PAIR + d, block, block, cell_dev(0, 0, 1))
+
+    def loading_tile(era, t):
+        steps = range(4 * t - NEAR, 4 * t - NEAR + 4)
+        for step in steps:
+            arrived(era, GV_PAIR + (-step) % Z, vbuf.at[era, (z + step + Z) % Z, 1 - yl])
+        packed = jnp.concatenate([vbuf[era, (z + step + Z) % Z] for step in steps], axis=0)
+        assemble(packed, t * TILE, v_eta, v_sum, gene_cols, False)
+
+    def assemble(packed, first_row, eta, total, columns, scale):
+        rows = pl.ds(pl.multiple_of(first_row, TILE), TILE)
         plain_h, plain_l = split(packed)
         square_h, square_l = split(packed * packed)
-        n = rows // 2
 
         def put(ref, column, left, right):
-            first, second = pairs(left, right)
-            both = jnp.concatenate([first.astype(BF16), second.astype(BF16)], axis=1)
-            ref[:, column:column + 128] = both.reshape(ref.shape[0], 128)
+            both = jnp.concatenate([half.astype(BF16) for half in pairs(left, right)], axis=1)
+            ref[rows, column:column + 128] = both.reshape(TILE, 128)
 
         put(total, 0, plain_h, square_h)
         put(total, 128, plain_l, square_l)
-        mask = left_half(columns.shape)
         if scale:
             high, low = split(packed * LOG2E)
             put(eta, 0, high, low)
@@ -208,43 +212,61 @@
         else:
             put(eta, 0, plain_h, plain_h)
             third = plain_l
-        first, second = pairs(third, third)
-        both = jnp.concatenate([first, second], axis=1).reshape(eta.shape[0], 128)
-        eta[:, 128:] = jnp.where(mask, both, columns[...]).astype(BF16)
-
-    def assemble_u(era):
-        assemble(ubuf[era].reshape(X * YH * CO, UROWS // 2, 128), UROWS, u_eta, u_sum, cell_cols, True)
-
-    def assemble_v(era):
-        assemble(vbuf[era].reshape(ZG * ZL * YL, VROWS // 2, 128), VROWS, v_eta, v_sum, gene_cols, False)
-
-    def sums(row_eta, column_eta, weights, count_ref, first, rows):
+        both = jnp.concatenate(pairs(third, third), axis=1).reshape(TILE, 128)
+        eta[rows, 128:] = jnp.where(left_half(both.shape), both, columns[rows, :]).astype(BF16)
+
+    def tile_sums(row_eta, column_eta, weights, count_ref, first, rows, tile):
         here = pl.ds(pl.multiple_of(first, rows), rows)
+        there = pl.ds(pl.multiple_of(tile * TILE, TILE), TILE)
         eta = lax.dot_general(
-            row_eta[here, :], column_eta[...], (((1,), (1,)), ((), ())), preferred_element_type=F32
+            row_eta, column_eta[there, :], (((1,), (1,)), ((), ())), preferred_element_type=F32
         )
         means = jnp.exp2(eta)
         high = means.astype(BF16)
         low = (means - high.astype(F32)).astype(BF16)
-        w = weights[...]
+        w = weights[there, :]
         acc = jnp.dot(high, w, preferred_element_type=F32) + jnp.dot(low, w, preferred_element_type=F32)
-        seen = jnp.dot(count_ref[here, :], w, preferred_element_type=F32)
-        total = acc[:, :128] + acc[:, 128:]
-        seen = seen[:, :128] + seen[:, 128:]
+        return acc, jnp.dot(count_ref[here, there], w, preferred_element_type=F32)
+
+    def add(first, second):
+        return second if first is None else (first[0] + second[0], first[1] + second[1])
+
+    def folded(sums):
+        total, seen = (part[:, :128] + part[:, 128:] for part in sums)
         return total - jnp.where(left_half(seen.shape), seen, 0.0)
 
     def updated(own, total):
         return own - STEP_CAP * jnp.tanh((total / (swap(total) + EPSILON)) / STEP_CAP)
 
+    def factor_part(it, j, sums):
+        there = (x + far_first(j)) % X
+        part_u[it, there] = folded(sums).reshape(YH, CO, UROWS, 128)
+        send(it, U_CORE + j, part_u.at[it, there, :, 1 - co], core_in.at[it, j], gene_dev(0, 0, 1))
+
+    def factor_tile_sums(j, tile):
+        first = ((x + far_first(j)) % X) * UCHUNK
+        rows = u_eta[pl.ds(pl.multiple_of(first, UCHUNK), UCHUNK), :]
+        return tile_sums(rows, v_eta, v_sum, cnt, first, UCHUNK, tile)
+
     def factor_step(it):
+        sums = None
+        gather_v_forward(it, 1, 5)
+        loading_tile(it, 0)
+        sums = add(sums, factor_tile_sums(0, 0))
+        gather_v_forward(it, 6, Z // 2)
+        for t in (1, 3, 2):
+            loading_tile(it, t)
+            sums = add(sums, factor_tile_sums(0, t))
+        factor_part(it, 0, sums)
+
         def chunk(j, carry):
-            there = (x + far_first(j)) % X
-            out = sums(u_eta, v_eta, v_sum, cnt, there * UCHUNK, UCHUNK)
-            part_u[it, there] = out.reshape(YH, CO, UROWS, 128)
-            send(it, U_CORE + j, part_u.at[it, there, :, 1 - co], core_in.at[it, j], gene_dev(0, 0, 1))
+            sums = None
+            for t in range(GENES // TILE):
+                sums = add(sums, factor_tile_sums(j, t))
+            factor_part(it, j, sums)
             return carry
 
-        lax.fori_loop(0, X, chunk, 0)
+        lax.fori_loop(1, X, chunk, 0)
         for j, dx in enumerate(FAR_FIRST):
             there = (x + dx) % X
             started.append((it, U_CORE + j, core_in.at[it, j]))
@@ -261,15 +283,33 @@
             total = total + chip_in[it, slot]
         own_u[...] = updated(own_u[...], total)
 
+    def loading_part(it, j, sums):
+        there = (zg + far_first(j)) % ZG
+        part_v[it, there] = folded(sums).reshape(ZL, YL, VROWS, 128)
+        send(it, V_PAIR + j, part_v.at[it, there, :, 1 - yl], pair_in.at[it, j], cell_dev(0, 0, 1))
+
+    def loading_tile_sums(j, tile):
+        there = (zg + far_first(j)) % ZG
+        places = [((there * ZL + k + NEAR + Z - z) % Z) * ZROWS for k in range(ZL)]
+        rows = jnp.concatenate([v_eta[pl.ds(pl.multiple_of(p, ZROWS), ZROWS), :] for p in places], axis=0)
+        return tile_sums(rows, u_eta, u_sum, cnt_t, there * VCHUNK, VCHUNK, tile)
+
     def loading_step(it):
+        sums = None
+        gather_u_forward(it + 1)
+        for dx in (0, 1, 3, 2):
+            there = factor_tile(it + 1, dx)
+            sums = add(sums, loading_tile_sums(0, there))
+        loading_part(it, 0, sums)
+
         def chunk(j, carry):
-            there = (zg + far_first(j)) % ZG
-            out = sums(v_eta, u_eta, u_sum, cnt_t, there * VCHUNK, VCHUNK)
-            part_v[it, there] = out.reshape(ZL, YL, VROWS, 128)
-            send(it, V_PAIR + j, part_v.at[it, there, :, 1 - yl], pair_in.at[it, j], cell_dev(0, 0, 1))
+            sums = None
+            for t in range(CELLS // TILE):
+                sums = add(sums, loading_tile_sums(j, t))
+            loading_part(it, j, sums)
             return carry
 
-        lax.fori_loop(0, ZG, chunk, 0)
+        lax.fori_loop(1, ZG, chunk, 0)
         for j, dg in enumerate(FAR_FIRST):
             there = (zg + dg) % ZG
             started.append((it, V_PAIR + j, pair_in.at[it, j]))
@@ -290,38 +330,34 @@
             total = total + ring_in[it, dg]
         own_v[...] = updated(own_v[...], total)
 
+    turn = ((NEAR + Z - z) * ZROWS) % GENES
     gather_v_start(0)
     gather_u_start(0)
-    offset_columns(cell_ref[...] * LOG2E, RANK, RANK + 3, cell_cols)
-    offset_columns(gene_ref[...] * LOG2E, RANK + 3, RANK, gene_cols)
+    offset_columns(cell_ref[...] * LOG2E, RANK, RANK + 3, None, cell_cols)
+    offset_columns(gene_ref[...] * LOG2E, RANK + 3, RANK, turn, gene_cols)
 
     def prepare(k, carry):
         load(k).wait()
         rows = pl.ds(pl.multiple_of(k * 256, 256), 256)
         block = cnt32[rows, :].astype(F32)
-        cnt[rows, :] = block.astype(BF16)
+        cnt[rows, :] = pltpu.roll(block, turn, axis=1).astype(BF16)
         cnt_t[:, rows] = block.T.astype(BF16)
         return carry
 
-    gather_u_finish(0)
     lax.fori_loop(0, CELLS // 256, prepare, 0)
-    gather_v_finish(0)
-    assemble_u(0)
-    assemble_v(0)
+    gather_u_forward(0)
+    for dx in (0, 1, 3, 2):
+        factor_tile(0, dx)
     for it in range(ITERS):
         factor_step(it)
-        ubuf[it + 1, chip, co] = pack(own_u[...])
+        ubuf[it + 1, x, yh, co] = pack(own_u[...])
         if it + 1 == ITERS:
             new_rows[:UROWS] = own_u[...]
         gather_u_start(it + 1)
-        gather_u_finish(it + 1)
-        assemble_u(it + 1)
         loading_step(it)
         if it + 1 < ITERS:
             vbuf[it + 1, z, yl] = pack(own_v[...])
             gather_v_start(it + 1)
-            gather_v_finish(it + 1)
-            assemble_v(it + 1)
     new_rows[UROWS:] = own_v[...]
     for era, slot, src in started:
         pltpu.make_async_remote_copy(
@@ -331,6 +367,7 @@
 
 
 def per_device(counts, factors, loadings, cell_offset, gene_offset):
+    arrays = (counts, factors, loadings, cell_offset.reshape(1, -1), gene_offset.reshape(1, -1))
     vmem = pl.BlockSpec(memory_space=pltpu.VMEM)
     hbm = pl.BlockSpec(memory_space=pltpu.HBM)
     scratch = [
@@ -349,7 +386,7 @@
         pltpu.VMEM((GENES, 128), F32),
         pltpu.VMEM((UROWS, 128), F32),
         pltpu.VMEM((VROWS, 128), F32),
-        pltpu.VMEM((ITERS + 1, X * YH, CO, UROWS // 2, 128), F32),
+        pltpu.VMEM((ITERS + 1, X, YH, CO, UROWS // 2, 128), F32),
         pltpu.VMEM((ITERS, Z, YL, VROWS // 2, 128), F32),
         pltpu.VMEM((ITERS, X, YH, CO, UROWS, 128), F32),
         pltpu.VMEM((ITERS, X, YH, UROWS, 128), F32),
@@ -373,9 +410,9 @@
         out_specs=vmem,
         scratch_shapes=scratch,
         compiler_params=pltpu.CompilerParams(
-            collective_id=0, has_side_effects=True, vmem_limit_bytes=63 * 1024 * 1024
+            collective_id=0, has_side_effects=True, vmem_limit_bytes=48 * 1024 * 1024
         ),
-    )(counts, factors, loadings, cell_offset.reshape(1, -1), gene_offset.reshape(1, -1))
+    )(*(pltpu.with_memory_space_constraint(a, pltpu.HBM) for a in arrays))
     return rows[:UROWS, :RANK], rows[UROWS:, :RANK]
 
 

time: 115 us -> 115 us (level)
  Pallas kernels: 111 us -> 113 us
  local copies, waits for them, and re-layouts: 2.7 us -> 1.22 us
    pallas_call x1, Pallas kernels: 111 us -> 113 us  [per_device(): pl.pallas_call(kernel, name='sweeps', out_shape=jax.ShapeDtypeStruct((URO...]
    slice x2, local copies, waits for them, and re-layouts: 2.7 us -> 1.22 us  [per_device(): return (rows[:UROWS, :RANK], rows[UROWS:, :RANK])]
where the time goes in v3:
time: 115 us
  Pallas kernels  113 us (98%)
  local copies, waits for them, and re-layouts  1.22 us (1%)
    pallas_call x1, Pallas kernels, per_device(): pl.pallas_call(kernel, name='sweeps', out_shape=jax.ShapeDtypeStruct((URO...  113 us

profile of v3, /device:TPU:1, one launch (start us, length us, event | category | flops | bytes accessed | tf_op | source)
XLA Modules:
  0.0 114.7 jit_solution(8288545347594759595)
XLA Ops:
  0.6 112.8 %sweeps.1 = f32[96,128]{1,0:T(8,128)S(1)} custom-call(s32[1024,1024]{1,0:T(8,128)} %counts_hbm.1, f32[64,64]{1,0:T(8,128)} %u_hbm.1, f32[32,64]{1,0:T(8,128)} %v_hbm.1, f32[1,1024]{1,0:T(1,128)} %bitcast.2, f32[1,1024]{1,0:T(1,128)} %bitcast.3), custom_call_target="tpu_custom_call" | custom-call | tf_op jit(solution)/shard_map/sweeps/pallas_call | solution.py:405
  113.4 0.6 slice.7
  114.0 0.6 slice.6

commit v4 on v3

--- a/solution.py
+++ b/solution.py
@@ -30,7 +30,7 @@
 U_CORE = 0
 U_CHIP = U_CORE + X
 V_PAIR = U_CHIP + X * YH
-V_LINE = V_PAIR + ZG
+V_LINE = V_PAIR + ZG * ZL
 V_RING = V_LINE + ZG * ZL
 GU_CHIP = V_RING + ZG
 GU_CORE = GU_CHIP + X * YH
@@ -57,10 +57,6 @@
     first = jnp.where(mask, left, swap(right))
     second = jnp.where(mask, swap(left), right)
     return first, second
-
-
-def far_first(j):
-    return (2 + 3 * j - (j * (j - 1)) // 2) % 4
 
 
 def kernel(
@@ -111,15 +107,12 @@
 
     started = []
 
-    def send(era, slot, src, dst, device):
+    def sent(era, slot, src, dst, device):
         copy = pltpu.make_async_remote_copy(
             src_ref=src, dst_ref=dst, send_sem=send_sem.at[era, slot],
             recv_sem=recv_sem.at[era, slot], device_id=device, device_id_type=MESH,
         )
         copy.start()
-
-    def sent(era, slot, src, dst, device):
-        send(era, slot, src, dst, device)
         started.append((era, slot, src))
 
     def arrived(era, slot, ref):
@@ -215,61 +208,46 @@
         both = jnp.concatenate(pairs(third, third), axis=1).reshape(TILE, 128)
         eta[rows, 128:] = jnp.where(left_half(both.shape), both, columns[rows, :]).astype(BF16)
 
-    def tile_sums(row_eta, column_eta, weights, count_ref, first, rows, tile):
+    def products(row_eta, column_eta, weights, count_ref, first, rows, columns):
         here = pl.ds(pl.multiple_of(first, rows), rows)
-        there = pl.ds(pl.multiple_of(tile * TILE, TILE), TILE)
         eta = lax.dot_general(
-            row_eta, column_eta[there, :], (((1,), (1,)), ((), ())), preferred_element_type=F32
+            row_eta, column_eta[columns, :], (((1,), (1,)), ((), ())), preferred_element_type=F32
         )
         means = jnp.exp2(eta)
         high = means.astype(BF16)
         low = (means - high.astype(F32)).astype(BF16)
-        w = weights[there, :]
-        acc = jnp.dot(high, w, preferred_element_type=F32) + jnp.dot(low, w, preferred_element_type=F32)
-        return acc, jnp.dot(count_ref[here, there], w, preferred_element_type=F32)
-
-    def add(first, second):
-        return second if first is None else (first[0] + second[0], first[1] + second[1])
+        stacked = jnp.concatenate([high, low, count_ref[here, columns]], axis=0)
+        return jnp.dot(stacked, weights[columns, :], preferred_element_type=F32)
 
     def folded(sums):
-        total, seen = (part[:, :128] + part[:, 128:] for part in sums)
-        return total - jnp.where(left_half(seen.shape), seen, 0.0)
+        high, low, seen = (part[:, :128] + part[:, 128:] for part in jnp.split(sums, 3, axis=0))
+        return high + low - jnp.where(left_half(seen.shape), seen, 0.0)
 
     def updated(own, total):
         return own - STEP_CAP * jnp.tanh((total / (swap(total) + EPSILON)) / STEP_CAP)
 
     def factor_part(it, j, sums):
-        there = (x + far_first(j)) % X
+        there = (x + FAR_FIRST[j]) % X
         part_u[it, there] = folded(sums).reshape(YH, CO, UROWS, 128)
-        send(it, U_CORE + j, part_u.at[it, there, :, 1 - co], core_in.at[it, j], gene_dev(0, 0, 1))
-
-    def factor_tile_sums(j, tile):
-        first = ((x + far_first(j)) % X) * UCHUNK
+        sent(it, U_CORE + j, part_u.at[it, there, :, 1 - co], core_in.at[it, j], gene_dev(0, 0, 1))
+
+    def factor_products(j, columns):
+        first = ((x + FAR_FIRST[j]) % X) * UCHUNK
         rows = u_eta[pl.ds(pl.multiple_of(first, UCHUNK), UCHUNK), :]
-        return tile_sums(rows, v_eta, v_sum, cnt, first, UCHUNK, tile)
+        return products(rows, v_eta, v_sum, cnt, first, UCHUNK, columns)
 
     def factor_step(it):
+        gather_v_forward(it, 1, Z // 2)
         sums = None
-        gather_v_forward(it, 1, 5)
-        loading_tile(it, 0)
-        sums = add(sums, factor_tile_sums(0, 0))
-        gather_v_forward(it, 6, Z // 2)
-        for t in (1, 3, 2):
+        for t in (0, 1, 3, 2):
             loading_tile(it, t)
-            sums = add(sums, factor_tile_sums(0, t))
+            part = factor_products(0, pl.ds(t * TILE, TILE))
+            sums = part if sums is None else sums + part
         factor_part(it, 0, sums)
-
-        def chunk(j, carry):
-            sums = None
-            for t in range(GENES // TILE):
-                sums = add(sums, factor_tile_sums(j, t))
-            factor_part(it, j, sums)
-            return carry
-
-        lax.fori_loop(1, X, chunk, 0)
+        for j in range(1, X):
+            factor_part(it, j, factor_products(j, pl.ds(0, GENES)))
         for j, dx in enumerate(FAR_FIRST):
             there = (x + dx) % X
-            started.append((it, U_CORE + j, core_in.at[it, j]))
             arrived(it, U_CORE + j, core_in.at[it, j])
             sum_u[it, j] = part_u[it, there, :, co] + core_in[it, j]
             for dh in (1, 0):
@@ -284,41 +262,33 @@
         own_u[...] = updated(own_u[...], total)
 
     def loading_part(it, j, sums):
-        there = (zg + far_first(j)) % ZG
+        there = (zg + FAR_FIRST[j]) % ZG
         part_v[it, there] = folded(sums).reshape(ZL, YL, VROWS, 128)
-        send(it, V_PAIR + j, part_v.at[it, there, :, 1 - yl], pair_in.at[it, j], cell_dev(0, 0, 1))
-
-    def loading_tile_sums(j, tile):
-        there = (zg + far_first(j)) % ZG
+        for d in (2, 3, 1, 0):
+            piece = part_v.at[it, there, (zl + d) % ZL, 1 - yl]
+            sent(it, V_PAIR + j * ZL + d, piece, pair_in.at[it, j, d], cell_dev(0, 0, 1))
+
+    def loading_products(j):
+        there = (zg + FAR_FIRST[j]) % ZG
         places = [((there * ZL + k + NEAR + Z - z) % Z) * ZROWS for k in range(ZL)]
         rows = jnp.concatenate([v_eta[pl.ds(pl.multiple_of(p, ZROWS), ZROWS), :] for p in places], axis=0)
-        return tile_sums(rows, u_eta, u_sum, cnt_t, there * VCHUNK, VCHUNK, tile)
+        return products(rows, u_eta, u_sum, cnt_t, there * VCHUNK, VCHUNK, pl.ds(0, CELLS))
 
     def loading_step(it):
-        sums = None
         gather_u_forward(it + 1)
         for dx in (0, 1, 3, 2):
-            there = factor_tile(it + 1, dx)
-            sums = add(sums, loading_tile_sums(0, there))
-        loading_part(it, 0, sums)
-
-        def chunk(j, carry):
-            sums = None
-            for t in range(CELLS // TILE):
-                sums = add(sums, loading_tile_sums(j, t))
-            loading_part(it, j, sums)
-            return carry
-
-        lax.fori_loop(1, ZG, chunk, 0)
+            factor_tile(it + 1, dx)
+        for j in range(ZG):
+            loading_part(it, j, loading_products(j))
         for j, dg in enumerate(FAR_FIRST):
             there = (zg + dg) % ZG
-            started.append((it, V_PAIR + j, pair_in.at[it, j]))
-            arrived(it, V_PAIR + j, pair_in.at[it, j])
-            sum1[it, j] = part_v[it, there, :, yl] + pair_in[it, j]
-            for d in (3, 2, 1):
-                sent(it, V_LINE + j * ZL + d, sum1.at[it, j, (zl + d) % ZL], line_in.at[it, j, d], cell_dev(0, d, 0))
+            for d in (2, 3, 1, 0):
+                arrived(it, V_PAIR + j * ZL + d, pair_in.at[it, j, d])
+                sum1[it, j, d] = part_v[it, there, (zl + d) % ZL, yl] + pair_in[it, j, d]
+                if d:
+                    sent(it, V_LINE + j * ZL + d, sum1.at[it, j, d], line_in.at[it, j, d], cell_dev(0, d, 0))
         for j, dg in enumerate(FAR_FIRST):
-            total = sum1[it, j, zl]
+            total = sum1[it, j, 0]
             for d in (1, 2, 3):
                 arrived(it, V_LINE + j * ZL + d, line_in.at[it, j, d])
                 total = total + line_in[it, j, d]

time: 115 us -> 117 us (1.017)
    pallas_call x1, Pallas kernels: 113 us -> 114 us  [per_device(): pl.pallas_call(kernel, name='sweeps', out_shape=jax.ShapeDtypeStruct((URO...]
where the time goes in v4:
time: 117 us; the launch traced here: 116 us
  Pallas kernels  114 us (97%)
  local copies, waits for them, and re-layouts  1.22 us (1%)
    pallas_call x1, Pallas kernels, per_device(): pl.pallas_call(kernel, name='sweeps', out_shape=jax.ShapeDtypeStruct((URO...  114 us

profile of v4, /device:TPU:1, one launch (start us, length us, event | category | flops | bytes accessed | tf_op | source)
XLA Modules:
  0.0 116.3 jit_solution(17628113551605916929)
XLA Ops:
  0.6 114.5 %sweeps.1 = f32[96,128]{1,0:T(8,128)S(1)} custom-call(s32[1024,1024]{1,0:T(8,128)} %counts_hbm.1, f32[64,64]{1,0:T(8,128)} %u_hbm.1, f32[32,64]{1,0:T(8,128)} %v_hbm.1, f32[1,1024]{1,0:T(1,128)} %bitcast.2, f32[1,1024]{1,0:T(1,128)} %bitcast.3), custom_call_target="tpu_custom_call" | custom-call | tf_op jit(solution)/shard_map/sweeps/pallas_call | solution.py:375
  115.1 0.6 slice.7
  115.7 0.6 slice.6

commit v5 on v2

--- a/solution.py
+++ b/solution.py
@@ -24,10 +24,11 @@
 UCHUNK = YH * CO * UROWS
 VCHUNK = ZL * YL * VROWS
 FAR_FIRST = (2, 1, 3, 0)
+TILE = 256
 U_CORE = 0
 U_CHIP = U_CORE + X
 V_PAIR = U_CHIP + X * YH
-V_LINE = V_PAIR + ZG
+V_LINE = V_PAIR + ZG * ZL
 V_RING = V_LINE + ZG * ZL
 GU_CHIP = V_RING + ZG
 GU_CORE = GU_CHIP + X * YH
@@ -56,11 +57,8 @@
     return first, second
 
 
-def unpack_to(ref, column, block, left, right):
-    first, second = pairs(left, right)
-    n = first.shape[-2]
-    ref[pl.ds(block, n), pl.ds(column, 128)] = first.astype(BF16)
-    ref[pl.ds(block + n, n), pl.ds(column, 128)] = second.astype(BF16)
+def near_first(t):
+    return t + t // 2 - 2 * (t // 3)
 
 
 def far_first(j):
@@ -126,6 +124,18 @@
         send(era, slot, src, dst, device)
         started.append((era, slot, src))
 
+    def take():
+        pending = list(started)
+        started.clear()
+        return pending
+
+    def drain(pending):
+        for era, slot, src in pending:
+            pltpu.make_async_remote_copy(
+                src_ref=src, dst_ref=src, send_sem=send_sem.at[era, slot],
+                recv_sem=recv_sem.at[era, slot], device_id=(c, g), device_id_type=MESH,
+            ).wait_send()
+
     def arrived(era, slot, ref):
         pltpu.make_async_remote_copy(
             src_ref=ref, dst_ref=ref, send_sem=send_sem.at[era, slot],
@@ -153,25 +163,33 @@
             rows = jnp.where(index == first_one + k, 1.0, rows)
         out[...] = rows.T
 
-    ubuf[0, chip, co] = pack(own_u[...])
+    ubuf[0, x, yh, co] = pack(own_u[...])
     vbuf[0, z, yl] = pack(own_v[...])
     pl.semaphore_wait(barrier, len(peers))
 
     def gather_u_start(era):
-        mine = ubuf.at[era, chip, co]
+        mine = ubuf.at[era, x, yh, co]
         for dx, dh in chips:
             sent(era, GU_CHIP + dx * YH + dh, mine, mine, gene_dev(dx, dh, 0))
         sent(era, GU_CORE, mine, mine, gene_dev(0, 0, 1))
 
-    def gather_u_finish(era):
-        order = [(1, 0), (3, 0), (0, 1), (2, 0), (1, 1), (3, 1), (2, 1)]
-        for dx, dh in order:
-            block = ubuf.at[era, ((x - dx) % X) * YH + (yh - dh) % YH, co]
+    def gather_u_forward(era):
+        for dx, dh in [(1, 0), (3, 0), (0, 1), (2, 0), (1, 1), (3, 1), (2, 1)]:
+            block = ubuf.at[era, (x - dx) % X, (yh - dh) % YH, co]
             arrived(era, GU_CHIP + dx * YH + dh, block)
             sent(era, GU_CORE + dx * YH + dh, block, block, gene_dev(0, 0, 1))
-        for dx, dh in [(0, 0)] + order:
-            block = ubuf.at[era, ((x - dx) % X) * YH + (yh - dh) % YH, 1 - co]
-            arrived(era, GU_CORE + dx * YH + dh, block)
+
+    def gather_u_finish(era):
+        def tile(t, carry):
+            dx = near_first(t)
+            there = (x - dx + X) % X
+            for dh in range(YH):
+                arrived(era, GU_CORE + dx * YH + dh, ubuf.at[era, there, (yh - dh) % YH, 1 - co])
+            packed = ubuf[era, there].reshape(YH * CO, UROWS // 2, 128)
+            assemble(packed, there * TILE, u_eta, u_sum, cell_cols, True)
+            return carry
+
+        lax.fori_loop(0, X, tile, 0)
 
     def gather_v_start(era):
         mine = vbuf.at[era, z, yl]
@@ -179,28 +197,35 @@
             sent(era, GV_Z + d, mine, mine, z_dev(d))
         sent(era, GV_PAIR, mine, mine, cell_dev(0, 0, 1))
 
-    def gather_v_finish(era):
-        near = [d for d in reversed(far)]
-        for d in near:
+    def gather_v_forward(era):
+        for d in reversed(far):
             block = vbuf.at[era, (z - d) % Z, yl]
             arrived(era, GV_Z + d, block)
             sent(era, GV_PAIR + d, block, block, cell_dev(0, 0, 1))
-        for d in [0] + near:
-            arrived(era, GV_PAIR + d, vbuf.at[era, (z - d) % Z, 1 - yl])
-
-    def assemble(packed, rows, eta, total, columns, scale):
+
+    def gather_v_finish(era):
+        def tile(t, carry):
+            there = (zg + near_first(t)) % ZG
+            for k in range(ZL):
+                source = there * ZL + k
+                arrived(era, GV_PAIR + (z - source + Z) % Z, vbuf.at[era, source, 1 - yl])
+            packed = vbuf[era, pl.ds(there * ZL, ZL)].reshape(ZL * YL, VROWS // 2, 128)
+            assemble(packed, there * TILE, v_eta, v_sum, gene_cols, False)
+            return carry
+
+        lax.fori_loop(0, ZG, tile, 0)
+
+    def assemble(packed, first_row, eta, total, columns, scale):
+        rows = pl.ds(pl.multiple_of(first_row, TILE), TILE)
         plain_h, plain_l = split(packed)
         square_h, square_l = split(packed * packed)
-        n = rows // 2
 
         def put(ref, column, left, right):
-            first, second = pairs(left, right)
-            both = jnp.concatenate([first.astype(BF16), second.astype(BF16)], axis=1)
-            ref[:, column:column + 128] = both.reshape(ref.shape[0], 128)
+            both = jnp.concatenate([half.astype(BF16) for half in pairs(left, right)], axis=1)
+            ref[rows, column:column + 128] = both.reshape(TILE, 128)
 
         put(total, 0, plain_h, square_h)
         put(total, 128, plain_l, square_l)
-        mask = left_half(columns.shape)
         if scale:
             high, low = split(packed * LOG2E)
             put(eta, 0, high, low)
@@ -208,15 +233,8 @@
         else:
             put(eta, 0, plain_h, plain_h)
             third = plain_l
-        first, second = pairs(third, third)
-        both = jnp.concatenate([first, second], axis=1).reshape(eta.shape[0], 128)
-        eta[:, 128:] = jnp.where(mask, both, columns[...]).astype(BF16)
-
-    def assemble_u(era):
-        assemble(ubuf[era].reshape(X * YH * CO, UROWS // 2, 128), UROWS, u_eta, u_sum, cell_cols, True)
-
-    def assemble_v(era):
-        assemble(vbuf[era].reshape(ZG * ZL * YL, VROWS // 2, 128), VROWS, v_eta, v_sum, gene_cols, False)
+        both = jnp.concatenate(pairs(third, third), axis=1).reshape(TILE, 128)
+        eta[rows, 128:] = jnp.where(left_half(both.shape), both, columns[rows, :]).astype(BF16)
 
     def sums(row_eta, column_eta, weights, count_ref, first, rows):
         here = pl.ds(pl.multiple_of(first, rows), rows)
@@ -226,12 +244,10 @@
         means = jnp.exp2(eta)
         high = means.astype(BF16)
         low = (means - high.astype(F32)).astype(BF16)
-        w = weights[...]
-        acc = jnp.dot(high, w, preferred_element_type=F32) + jnp.dot(low, w, preferred_element_type=F32)
-        seen = jnp.dot(count_ref[here, :], w, preferred_element_type=F32)
-        total = acc[:, :128] + acc[:, 128:]
-        seen = seen[:, :128] + seen[:, 128:]
-        return total - jnp.where(left_half(seen.shape), seen, 0.0)
+        stacked = jnp.concatenate([high, low, count_ref[here, :]], axis=0)
+        out = jnp.dot(stacked, weights[...], preferred_element_type=F32)
+        high, low, seen = (part[:, :128] + part[:, 128:] for part in jnp.split(out, 3, axis=0))
+        return high + low - jnp.where(left_half(seen.shape), seen, 0.0)
 
     def updated(own, total):
         return own - STEP_CAP * jnp.tanh((total / (swap(total) + EPSILON)) / STEP_CAP)
@@ -266,25 +282,29 @@
             there = (zg + far_first(j)) % ZG
             out = sums(v_eta, u_eta, u_sum, cnt_t, there * VCHUNK, VCHUNK)
             part_v[it, there] = out.reshape(ZL, YL, VROWS, 128)
-            send(it, V_PAIR + j, part_v.at[it, there, :, 1 - yl], pair_in.at[it, j], cell_dev(0, 0, 1))
+            for d in (2, 3, 1, 0):
+                send(it, V_PAIR + j * ZL + d, part_v.at[it, there, (zl + d) % ZL, 1 - yl], pair_in.at[it, j, d], cell_dev(0, 0, 1))
             return carry
 
         lax.fori_loop(0, ZG, chunk, 0)
         for j, dg in enumerate(FAR_FIRST):
             there = (zg + dg) % ZG
-            started.append((it, V_PAIR + j, pair_in.at[it, j]))
-            arrived(it, V_PAIR + j, pair_in.at[it, j])
-            sum1[it, j] = part_v[it, there, :, yl] + pair_in[it, j]
-            for d in (3, 2, 1):
-                sent(it, V_LINE + j * ZL + d, sum1.at[it, j, (zl + d) % ZL], line_in.at[it, j, d], cell_dev(0, d, 0))
+            for d in (2, 3, 1, 0):
+                started.append((it, V_PAIR + j * ZL + d, pair_in.at[it, j, d]))
+                arrived(it, V_PAIR + j * ZL + d, pair_in.at[it, j, d])
+                sum1[it, j, d] = part_v[it, there, (zl + d) % ZL, yl] + pair_in[it, j, d]
+                if d:
+                    sent(it, V_LINE + j * ZL + d, sum1.at[it, j, d], line_in.at[it, j, d], cell_dev(0, d, 0))
+        pending = take()
         for j, dg in enumerate(FAR_FIRST):
-            total = sum1[it, j, zl]
+            total = sum1[it, j, 0]
             for d in (1, 2, 3):
                 arrived(it, V_LINE + j * ZL + d, line_in.at[it, j, d])
                 total = total + line_in[it, j, d]
             if dg:
                 sum2[it, j] = total
                 sent(it, V_RING + dg, sum2.at[it, j], ring_in.at[it, dg], cell_dev(dg, 0, 0))
+        drain(pending)
         for dg in (1, 3, 2):
             arrived(it, V_RING + dg, ring_in.at[it, dg])
             total = total + ring_in[it, dg]
@@ -303,34 +323,35 @@
         cnt_t[:, rows] = block.T.astype(BF16)
         return carry
 
+    lax.fori_loop(0, CELLS // 256, prepare, 0)
+    gather_u_forward(0)
+    gather_v_forward(0)
     gather_u_finish(0)
-    lax.fori_loop(0, CELLS // 256, prepare, 0)
     gather_v_finish(0)
-    assemble_u(0)
-    assemble_v(0)
     for it in range(ITERS):
         factor_step(it)
-        ubuf[it + 1, chip, co] = pack(own_u[...])
+        pending = take()
+        ubuf[it + 1, x, yh, co] = pack(own_u[...])
+        gather_u_start(it + 1)
         if it + 1 == ITERS:
             new_rows[:UROWS] = own_u[...]
-        gather_u_start(it + 1)
+        drain(pending)
+        gather_u_forward(it + 1)
         gather_u_finish(it + 1)
-        assemble_u(it + 1)
         loading_step(it)
         if it + 1 < ITERS:
+            pending = take()
             vbuf[it + 1, z, yl] = pack(own_v[...])
             gather_v_start(it + 1)
+            drain(pending)
+            gather_v_forward(it + 1)
             gather_v_finish(it + 1)
-            assemble_v(it + 1)
     new_rows[UROWS:] = own_v[...]
-    for era, slot, src in started:
-        pltpu.make_async_remote_copy(
-            src_ref=src, dst_ref=src, send_sem=send_sem.at[era, slot],
-            recv_sem=recv_sem.at[era, slot], device_id=(c, g), device_id_type=MESH,
-        ).wait_send()
+    drain(take())
 
 
 def per_device(counts, factors, loadings, cell_offset, gene_offset):
+    arrays = (counts, factors, loadings, cell_offset.reshape(1, -1), gene_offset.reshape(1, -1))
     vmem = pl.BlockSpec(memory_space=pltpu.VMEM)
     hbm = pl.BlockSpec(memory_space=pltpu.HBM)
     scratch = [
@@ -349,7 +370,7 @@
         pltpu.VMEM((GENES, 128), F32),
         pltpu.VMEM((UROWS, 128), F32),
         pltpu.VMEM((VROWS, 128), F32),
-        pltpu.VMEM((ITERS + 1, X * YH, CO, UROWS // 2, 128), F32),
+        pltpu.VMEM((ITERS + 1, X, YH, CO, UROWS // 2, 128), F32),
         pltpu.VMEM((ITERS, Z, YL, VROWS // 2, 128), F32),
         pltpu.VMEM((ITERS, X, YH, CO, UROWS, 128), F32),
         pltpu.VMEM((ITERS, X, YH, UROWS, 128), F32),
@@ -373,9 +394,9 @@
         out_specs=vmem,
         scratch_shapes=scratch,
         compiler_params=pltpu.CompilerParams(
-            collective_id=0, has_side_effects=True, vmem_limit_bytes=63 * 1024 * 1024
+            collective_id=0, has_side_effects=True, vmem_limit_bytes=48 * 1024 * 1024
         ),
-    )(counts, factors, loadings, cell_offset.reshape(1, -1), gene_offset.reshape(1, -1))
+    )(*(pltpu.with_memory_space_constraint(a, pltpu.HBM) for a in arrays))
     return rows[:UROWS, :RANK], rows[UROWS:, :RANK]
 
 

time: 115 us -> 110 us (0.957)
  Pallas kernels: 111 us -> 108 us
  local copies, waits for them, and re-layouts: 2.7 us -> 1.22 us
    pallas_call x1, Pallas kernels: 111 us -> 108 us  [per_device(): pl.pallas_call(kernel, name='sweeps', out_shape=jax.ShapeDtypeStruct((URO...]
    slice x2, local copies, waits for them, and re-layouts: 2.7 us -> 1.22 us  [per_device(): return (rows[:UROWS, :RANK], rows[UROWS:, :RANK])]
where the time goes in v5:
time: 110 us; the launch traced here: 109 us
  Pallas kernels  108 us (98%)
  local copies, waits for them, and re-layouts  1.22 us (1%)
    pallas_call x1, Pallas kernels, per_device(): pl.pallas_call(kernel, name='sweeps', out_shape=jax.ShapeDtypeStruct((URO...  108 us

profile of v5, /device:TPU:1, one launch (start us, length us, event | category | flops | bytes accessed | tf_op | source)
XLA Modules:
  0.0 109.4 jit_solution(5548982359475366509)
XLA Ops:
  0.6 107.5 %sweeps.1 = f32[96,128]{1,0:T(8,128)S(1)} custom-call(s32[1024,1024]{1,0:T(8,128)} %counts_hbm.1, f32[64,64]{1,0:T(8,128)} %u_hbm.1, f32[32,64]{1,0:T(8,128)} %v_hbm.1, f32[1,1024]{1,0:T(1,128)} %bitcast.2, f32[1,1024]{1,0:T(1,128)} %bitcast.3), custom_call_target="tpu_custom_call" | custom-call | tf_op jit(solution)/shard_map/sweeps/pallas_call | solution.py:389
  108.2 0.6 slice.7
  108.8 0.6 slice.6

commit v6 on v5

--- a/solution.py
+++ b/solution.py
@@ -24,6 +24,8 @@
 UCHUNK = YH * CO * UROWS
 VCHUNK = ZL * YL * VROWS
 FAR_FIRST = (2, 1, 3, 0)
+SHIFT = 2
+ZROWS = YL * VROWS
 TILE = 256
 U_CORE = 0
 U_CHIP = U_CORE + X
@@ -72,30 +74,28 @@
     part_v, pair_in, sum1, line_in, sum2, ring_in, load_sem, send_sem, recv_sem,
 ):
     c, g = lax.axis_index("cell"), lax.axis_index("gene")
-    z, yl = c // YL, c % YL
-    zg, zl = z // ZL, z % ZL
     chip, co = g // CO, g % CO
     x, yh = chip // YH, chip % YH
+    shift = SHIFT * co
+    z, yl = (c // YL + shift) % Z, c % YL
+    zg, zl = z // ZL, z % ZL
+    turn = shift * ZROWS
 
     def cell_dev(dg, dl, dy):
         there = ((zg + dg) % ZG) * ZL + (zl + dl) % ZL
-        return (there * YL + (yl + dy) % YL, g)
+        return (((there - shift + Z) % Z) * YL + (yl + dy) % YL, g)
 
     def gene_dev(dx, dh, dc):
         there = ((x + dx) % X) * YH + (yh + dh) % YH
         return (c, there * CO + (co + dc) % CO)
 
     def z_dev(d):
-        return (((z + d) % Z) * YL + yl, g)
+        return (((z + d - shift + Z) % Z) * YL + yl, g)
 
     far = [d for k in range(Z // 2, 0, -1) for d in dict.fromkeys((k, Z - k))]
     chips = [(dx, dh) for dx in FAR_FIRST for dh in (1, 0) if dx or dh]
     peers = [z_dev(d) for d in far] + [gene_dev(dx, dh, 0) for dx, dh in chips]
     peers += [cell_dev(0, 0, 1), gene_dev(0, 0, 1)]
-    barrier = pltpu.get_barrier_semaphore()
-    for peer in peers:
-        pl.semaphore_signal(barrier, inc=1, device_id=peer, device_id_type=MESH)
-
     def load(k):
         rows = pl.ds(k * 256, 256)
         return pltpu.make_async_copy(counts_hbm.at[rows], cnt32.at[rows], load_sem.at[k])
@@ -111,6 +111,10 @@
     for k in range(CELLS // 256):
         load(k).start()
 
+    barrier = pltpu.get_barrier_semaphore()
+    for peer in peers:
+        pl.semaphore_signal(barrier, inc=1, device_id=peer, device_id_type=MESH)
+
     started = []
 
     def send(era, slot, src, dst, device):
@@ -153,7 +157,7 @@
     own_u[:, :RANK] = u_ref[...]
     own_v[:, :RANK] = v_ref[...]
 
-    def offset_columns(row, first_offset, first_one, out):
+    def offset_columns(row, first_offset, first_one, turn, out):
         high, rest = split(row)
         mid, low = split(rest)
         index = lax.broadcasted_iota(jnp.int32, (128, row.shape[1]), 0)
@@ -161,7 +165,7 @@
         for k, part in enumerate((high, mid, low)):
             rows = jnp.where(index == first_offset + k, part, rows)
             rows = jnp.where(index == first_one + k, 1.0, rows)
-        out[...] = rows.T
+        out[...] = (rows if turn is None else pltpu.roll(rows, turn, axis=1)).T
 
     ubuf[0, x, yh, co] = pack(own_u[...])
     vbuf[0, z, yl] = pack(own_v[...])
@@ -253,23 +257,30 @@
         return own - STEP_CAP * jnp.tanh((total / (swap(total) + EPSILON)) / STEP_CAP)
 
     def factor_step(it):
+        def serve(j, steps):
+            dx = far_first(j)
+            arrived(it, U_CORE + j, core_in.at[it, j])
+            sum_u[it, j] = part_u[it, (x + dx) % X, :, co] + core_in[it, j]
+            for dh in steps:
+                slot = dx * YH + dh
+                send(it, U_CHIP + slot, sum_u.at[it, j, (yh + dh) % YH], chip_in.at[it, slot], gene_dev(dx, dh, 0))
+
         def chunk(j, carry):
             there = (x + far_first(j)) % X
             out = sums(u_eta, v_eta, v_sum, cnt, there * UCHUNK, UCHUNK)
             part_u[it, there] = out.reshape(YH, CO, UROWS, 128)
             send(it, U_CORE + j, part_u.at[it, there, :, 1 - co], core_in.at[it, j], gene_dev(0, 0, 1))
+
+            @pl.when(j > 0)
+            def _():
+                serve(j - 1, (1, 0))
+
             return carry
 
         lax.fori_loop(0, X, chunk, 0)
-        for j, dx in enumerate(FAR_FIRST):
-            there = (x + dx) % X
-            started.append((it, U_CORE + j, core_in.at[it, j]))
-            arrived(it, U_CORE + j, core_in.at[it, j])
-            sum_u[it, j] = part_u[it, there, :, co] + core_in[it, j]
-            for dh in (1, 0):
-                if dx or dh:
-                    slot = dx * YH + dh
-                    sent(it, U_CHIP + slot, sum_u.at[it, j, (yh + dh) % YH], chip_in.at[it, slot], gene_dev(dx, dh, 0))
+        serve(X - 1, (1,))
+        started.extend((it, U_CORE + j, core_in.at[it, j]) for j in range(X))
+        started.extend((it, U_CHIP + slot, chip_in.at[it, slot]) for slot in range(1, X * YH))
         total = sum_u[it, len(FAR_FIRST) - 1, yh]
         for dx, dh in [(1, 0), (3, 0), (0, 1), (2, 0), (1, 1), (3, 1), (2, 1)]:
             slot = dx * YH + dh
@@ -312,13 +323,13 @@
 
     gather_v_start(0)
     gather_u_start(0)
-    offset_columns(cell_ref[...] * LOG2E, RANK, RANK + 3, cell_cols)
-    offset_columns(gene_ref[...] * LOG2E, RANK + 3, RANK, gene_cols)
+    offset_columns(cell_ref[...] * LOG2E, RANK, RANK + 3, None, cell_cols)
+    offset_columns(gene_ref[...] * LOG2E, RANK + 3, RANK, turn, gene_cols)
 
     def prepare(k, carry):
         load(k).wait()
         rows = pl.ds(pl.multiple_of(k * 256, 256), 256)
-        block = cnt32[rows, :].astype(F32)
+        block = pltpu.roll(cnt32[rows, :].astype(F32), turn, axis=1)
         cnt[rows, :] = block.astype(BF16)
         cnt_t[:, rows] = block.T.astype(BF16)
         return carry

time: 110 us -> 109 us (level)
  no operation moved by 1% of the time
where the time goes in v6:
time: 109 us
  Pallas kernels  107 us (98%)
  local copies, waits for them, and re-layouts  1.22 us (1%)
    pallas_call x1, Pallas kernels, per_device(): pl.pallas_call(kernel, name='sweeps', out_shape=jax.ShapeDtypeStruct((URO...  107 us

profile of v6, /device:TPU:1, one launch (start us, length us, event | category | flops | bytes accessed | tf_op | source)
XLA Modules:
  0.0 108.7 jit_solution(13675107177243860707)
XLA Ops:
  0.6 106.8 %sweeps.1 = f32[96,128]{1,0:T(8,128)S(1)} custom-call(s32[1024,1024]{1,0:T(8,128)} %counts_hbm.1, f32[64,64]{1,0:T(8,128)} %u_hbm.1, f32[32,64]{1,0:T(8,128)} %v_hbm.1, f32[1,1024]{1,0:T(1,128)} %bitcast.2, f32[1,1024]{1,0:T(1,128)} %bitcast.3), custom_call_target="tpu_custom_call" | custom-call | tf_op jit(solution)/shard_map/sweeps/pallas_call | solution.py:400
  107.4 0.6 slice.7
  108.0 0.6 slice.6

commit v7 on v6

--- a/solution.py
+++ b/solution.py
@@ -25,6 +25,7 @@
 VCHUNK = ZL * YL * VROWS
 FAR_FIRST = (2, 1, 3, 0)
 SHIFT = 2
+REACH = Z // 4
 ZROWS = YL * VROWS
 TILE = 256
 U_CORE = 0
@@ -94,7 +95,8 @@
 
     far = [d for k in range(Z // 2, 0, -1) for d in dict.fromkeys((k, Z - k))]
     chips = [(dx, dh) for dx in FAR_FIRST for dh in (1, 0) if dx or dh]
-    peers = [z_dev(d) for d in far] + [gene_dev(dx, dh, 0) for dx, dh in chips]
+    near = [d for d in far if min(d, Z - d) <= REACH]
+    peers = [z_dev(d) for d in near] + [gene_dev(dx, dh, 0) for dx, dh in chips]
     peers += [cell_dev(0, 0, 1), gene_dev(0, 0, 1)]
     def load(k):
         rows = pl.ds(k * 256, 256)
@@ -197,14 +199,20 @@
 
     def gather_v_start(era):
         mine = vbuf.at[era, z, yl]
-        for d in far:
+        for d in far if era else near:
             sent(era, GV_Z + d, mine, mine, z_dev(d))
         sent(era, GV_PAIR, mine, mine, cell_dev(0, 0, 1))
 
     def gather_v_forward(era):
-        for d in reversed(far):
-            block = vbuf.at[era, (z - d) % Z, yl]
+        for d in list(reversed(far)) if era else near + list(reversed(far))[len(near):]:
+            block = vbuf.at[era, (z - d + Z) % Z, yl]
             arrived(era, GV_Z + d, block)
+            if not era and min(d, Z - d) == REACH:
+                for k in range(REACH, 0, -1):
+                    if d == REACH:
+                        sent(era, GV_Z + d + k, block, block, z_dev(k))
+                    elif d - k > Z // 2:
+                        sent(era, GV_Z + d - k, block, block, z_dev(Z - k))
             sent(era, GV_PAIR + d, block, block, cell_dev(0, 0, 1))
 
     def gather_v_finish(era):

time: 109 us -> 109 us (level)
  no operation moved by 1% of the time
where the time goes in v7:
time: 109 us
  Pallas kernels  107 us (98%)
  local copies, waits for them, and re-layouts  1.22 us (1%)
    pallas_call x1, Pallas kernels, per_device(): pl.pallas_call(kernel, name='sweeps', out_shape=jax.ShapeDtypeStruct((URO...  107 us

profile of v7, /device:TPU:1, one launch (start us, length us, event | category | flops | bytes accessed | tf_op | source)
XLA Modules:
  0.0 108.8 jit_solution(8366936034433225220)
XLA Ops:
  0.6 106.9 %sweeps.1 = f32[96,128]{1,0:T(8,128)S(1)} custom-call(s32[1024,1024]{1,0:T(8,128)} %counts_hbm.1, f32[64,64]{1,0:T(8,128)} %u_hbm.1, f32[32,64]{1,0:T(8,128)} %v_hbm.1, f32[1,1024]{1,0:T(1,128)} %bitcast.2, f32[1,1024]{1,0:T(1,128)} %bitcast.3), custom_call_target="tpu_custom_call" | custom-call | tf_op jit(solution)/shard_map/sweeps/pallas_call | solution.py:408
  107.5 0.6 slice.7
  108.1 0.6 slice.6
